TPU v7x, 128 devices: a whole 4x4x4 slice. The times are simulated.
128 devices in a mesh: row: 8 (over y_hi, z), col: 16 (over x, y_lo, core).
Axes of the slice: x: 4, y: 4 (y_hi: 2, y_lo: 2; y = y_hi * 2 + y_lo), z: 4, core: 2. Of those that a mesh axis runs over, the one named last changes fastest.
Arguments:
- a_vals: bfloat16 [128, 32, 128, 128], P('row', 'col'), may hold values from -0.21875 to 0.21875
- a_cols: int32 [128, 32], P('row', 'col'), may hold values from 0 to 127, as said below
- b_vals: bfloat16 [128, 48, 128, 128], P('row', 'col'), may hold values from -6 to 6
- b_cols: int32 [128, 48], P('row', 'col'), may hold values from 0 to 255, as said below
- c_cols: int32 [128, 128], P('row', 'col'), may hold values from 0 to 255, as said below
- c_send: int32 [8, 16, 128], P('row', 'col'), may hold values from 0 to 127, each once within a row
Outputs:
- c_owned: bfloat16 [16384, 128, 128], P(('row', 'col'))
Inputs may be any that keep to these rules, and one draw needn't show every extreme that they name: `a_cols`: the entries of block row i in slot group c are 2 distinct block columns of panel c, c * 8 to (c + 1) * 8 - 1. `b_cols`: the entries of block row k in slot group c are 3 distinct block columns c * 16 to (c + 1) * 16 - 1. `c_cols`: the entries of block row i in slot group c are 8 distinct block columns c * 16 to (c + 1) * 16 - 1.
All inputs are finite; a program needn't handle non-finite values.
Results may differ from a plain program's by a relative error of at most 0.001.
Values may be sent and summed in bfloat16 or wider, within the bound.
A program may use at most 384 MiB of HBM per device.

v0:
```python
import jax
import jax.numpy as jnp
from jax import lax
from jax.sharding import PartitionSpec as P

SBD = 16


def from_behind(shard, axis, by):
    length = lax.axis_size(axis)
    return lax.ppermute(shard, axis, [(i, (i + by) % length) for i in range(length)])


def on_device(a_vals, a_cols, b_vals, b_cols, c_cols, c_send):
    row_count = a_vals.shape[0]
    slot_count = a_vals.shape[1]
    block_len = a_vals.shape[2]
    col_index = lax.axis_index("col")
    col_count = lax.axis_size("col")
    local_cols = (b_cols - col_index * SBD).astype(jnp.bfloat16)
    b_whole, bcol_whole = (
        lax.all_gather(b_vals, "row", axis=0, tiled=True),
        lax.all_gather(local_cols, "row", axis=0, tiled=True),
    )
    bcol_whole = bcol_whole.astype(jnp.int32)
    panel_len = b_whole.shape[0] // col_count
    keep_local = c_cols - col_index * SBD
    a_offsets = (a_cols - col_index * panel_len).astype(jnp.bfloat16)
    zero_sum = jnp.zeros((row_count, keep_local.shape[1], block_len, block_len), jnp.float32)

    def accumulate(kept_sum, a_piece, off_piece, panel_ids):
        inner_rows = off_piece.astype(jnp.int32) + panel_ids[None, :] * panel_len
        b_chosen = jnp.take(b_whole, inner_rows, axis=0)
        col_chosen = jnp.take(bcol_whole, inner_rows, axis=0)
        matches = (col_chosen[:, :, :, None] == keep_local[:, None, None, :]).astype(jnp.bfloat16)
        selected = jnp.einsum(
            "ipqn,ipqbc->ipnbc", matches, b_chosen, preferred_element_type=jnp.bfloat16
        )
        return kept_sum + jnp.einsum(
            "ipab,ipnbc->inac", a_piece, selected, preferred_element_type=jnp.float32
        )

    def one_turn(step, carry):
        kept_sum, a_piece, off_piece = carry
        panel_now = (col_index - step) % col_count
        kept_sum = accumulate(
            kept_sum, a_piece, off_piece, jnp.full((slot_count,), panel_now, jnp.int32)
        )
        a_piece, off_piece = from_behind((a_piece, off_piece), "col", 1)
        return (kept_sum, a_piece, off_piece)

    kept_sum, a_last, off_last = lax.fori_loop(
        0, col_count - 1, one_turn, (zero_sum, a_vals, a_offsets)
    )
    panel_last = (col_index - (col_count - 1)) % col_count
    kept_sum = accumulate(
        kept_sum, a_last, off_last, jnp.full((slot_count,), panel_last, jnp.int32)
    )
    kept_blocks = kept_sum.astype(jnp.bfloat16).reshape(-1, block_len, block_len)
    send_order = c_send.reshape(-1)
    outgoing = jnp.take(kept_blocks, send_order, axis=0)
    return lax.all_to_all(outgoing, ("row", "col"), split_axis=0, concat_axis=0, tiled=True)


def solution(mesh):
    in_specs = (
        P("row", "col", None, None),
        P("row", "col"),
        P("row", "col", None, None),
        P("row", "col"),
        P("row", "col"),
        P("row", "col", None),
    )
    out_specs = P(("row", "col"), None, None)
    return jax.shard_map(
        on_device, mesh=mesh, in_specs=in_specs, out_specs=out_specs, check_vma=False
    )
```

profile of v0, /device:TPU:1, one launch (start us, length us, event | category | flops | bytes accessed | tf_op | source)
XLA Modules:
  0.0 709.6 jit_solution(17216143636868197633)
XLA Ops:
  8.5 21.8 %all-gather = bf16[8,16,3]{1,2,0:T(4,128)(2,1)S(1)} all-gather(bf16[1,16,3]{1,2,0:T(4,128)(2,1)S(1)} %fusion.26), channel_id=1, replica_groups=mesh['row'=8,'col'=16] {'row'}, dimensions={0}, use_global_device_ids=true | all-gather | bytes 864 | tf_op jit(solution)/shard_map/all_gather | solution.py:23
  33.2 123.5 %all-gather.3.cloned.1.call-done = bf16[128,3,128,128]{3,2,1,0:T(8,128)(2,1)} async-done(((bf16[16,3,128,128]{3,2,1,0:T(8,128)(2,1)}), bf16[128,3,128,128]{3,2,1,0:T(8,128)(2,1)}) %all-gather.3.cloned.1.call-update) | async-done | bytes 12582928 | tf_op jit(solution)/shard_map/all_gather | solution.py:22
  156.7 444.4 %while.20 = (s32[]{:T(128)}, f32[16,8,128,128]{2,3,1,0:T(8,128)}, bf16[16,2,128,128]{3,2,1,0:T(8,128)(2,1)S(1)}, bf16[16,2]{0,1:T(2,128)(2,1)S(1)}, s32[]{:T(128...) while((s32[]{:T(128)}, f32[16,8,128,128]{2,3,1,0:T(8,128)}, ...), condition=%wide.region_1.0_spmd.clone, body=%wide.region_0.3_spmd.clone.sunk | while | flops 1104677120 | bytes 50341760 | solution.py:52
  158.9 7.2 %gather_fusion = bf16[32,3,128,128]{3,2,1,0:T(8,128)(2,1)} fusion(bf16[128,3,128,128]{3,2,1,0:T(8,128)(2,1)} %get-tuple-element.344, s32[1024]{0:T(1024)S(1)} %pad_clamp_fusion.4), kind=kCustom, calls=%fused_computation.1.clone.clone.1 | custom fusion | bytes 6291584 | tf_op jit(solution)/shard_map/while/body/eval_jaxpr/jit(_take)/gather | solution.py:33
  167.1 7.9 %fusion.36 = bf16[16,2,8,128,128]{4,2,3,1,0:T(8,128)(2,1)} fusion(bf16[16,2,3,128,128]{4,3,2,1,0:T(8,128)(2,1)} %bitcast.56, pred[16,2]{1,0:T(8,128)(4,1)S(1)} %copy.91, s32[16,8]{1,0:T(8,128)S(1)} %get-tuple-element.343, s32[16,2,3]{2,1,0:T(2,128)S(1)} %copy.93), kind=kOutput, calls=%fused_computation.9.clone.1 | convolution fusion | flops 26739456 | bytes 11535264 | tf_op jit(solution)/shard_map/while/body/eval_jaxpr/ipqn,ipqbc->ipnbc/dot_general | solution.py:36
  175.0 9.3 %bitcast_add_fusion.3 = f32[16,8,128,128]{2,3,1,0:T(8,128)} fusion(f32[16,8,128,128]{2,3,1,0:T(8,128)} %get-tuple-element.325, pred[]{:T(512)S(6)} %compare.5, bf16[16,2,8,128,128]{4,2,3,1,0:T(8,128)(2,1)} %fusion.36, bf16[16,2,128,128]{3,2,1,0:T(8,128)(2,1)S(1)} %copy.100), kind=kOutput, calls=%fused_computation.5.clone.1 | convolution fusion | flops 1077936128 | bytes 26214400 | tf_op jit(solution)/shard_map/while/body/eval_jaxpr/ipab,ipnbc->inac/dot_general | solution.py:39
  187.3 7.2 %gather_fusion = bf16[32,3,128,128]{3,2,1,0:T(8,128)(2,1)} fusion(bf16[128,3,128,128]{3,2,1,0:T(8,128)(2,1)} %get-tuple-element.344, s32[1024]{0:T(1024)S(1)} %pad_clamp_fusion.4), kind=kCustom, calls=%fused_computation.1.clone.clone.1 | custom fusion | bytes 6291584 | tf_op jit(solution)/shard_map/while/body/eval_jaxpr/jit(_take)/gather | solution.py:33
  195.4 7.9 %fusion.36 = bf16[16,2,8,128,128]{4,2,3,1,0:T(8,128)(2,1)} fusion(bf16[16,2,3,128,128]{4,3,2,1,0:T(8,128)(2,1)} %bitcast.56, pred[16,2]{1,0:T(8,128)(4,1)S(1)} %copy.91, s32[16,8]{1,0:T(8,128)S(1)} %get-tuple-element.343, s32[16,2,3]{2,1,0:T(2,128)S(1)} %copy.93), kind=kOutput, calls=%fused_computation.9.clone.1 | convolution fusion | flops 26739456 | bytes 11535264 | tf_op jit(solution)/shard_map/while/body/eval_jaxpr/ipqn,ipqbc->ipnbc/dot_general | solution.py:36
  203.4 11.7 %bitcast_add_fusion.3 = f32[16,8,128,128]{2,3,1,0:T(8,128)} fusion(f32[16,8,128,128]{2,3,1,0:T(8,128)} %get-tuple-element.325, pred[]{:T(512)S(6)} %compare.5, bf16[16,2,8,128,128]{4,2,3,1,0:T(8,128)(2,1)} %fusion.36, bf16[16,2,128,128]{3,2,1,0:T(8,128)(2,1)S(1)} %copy.100), kind=kOutput, calls=%fused_computation.5.clone.1 | convolution fusion | flops 1077936128 | bytes 26214400 | tf_op jit(solution)/shard_map/while/body/eval_jaxpr/ipab,ipnbc->inac/dot_general | solution.py:39
  216.2 7.2 %gather_fusion = bf16[32,3,128,128]{3,2,1,0:T(8,128)(2,1)} fusion(bf16[128,3,128,128]{3,2,1,0:T(8,128)(2,1)} %get-tuple-element.344, s32[1024]{0:T(1024)S(1)} %pad_clamp_fusion.4), kind=kCustom, calls=%fused_computation.1.clone.clone.1 | custom fusion | bytes 6291584 | tf_op jit(solution)/shard_map/while/body/eval_jaxpr/jit(_take)/gather | solution.py:33
  224.4 7.9 %fusion.36 = bf16[16,2,8,128,128]{4,2,3,1,0:T(8,128)(2,1)} fusion(bf16[16,2,3,128,128]{4,3,2,1,0:T(8,128)(2,1)} %bitcast.56, pred[16,2]{1,0:T(8,128)(4,1)S(1)} %copy.91, s32[16,8]{1,0:T(8,128)S(1)} %get-tuple-element.343, s32[16,2,3]{2,1,0:T(2,128)S(1)} %copy.93), kind=kOutput, calls=%fused_computation.9.clone.1 | convolution fusion | flops 26739456 | bytes 11535264 | tf_op jit(solution)/shard_map/while/body/eval_jaxpr/ipqn,ipqbc->ipnbc/dot_general | solution.py:36
  232.4 11.7 %bitcast_add_fusion.3 = f32[16,8,128,128]{2,3,1,0:T(8,128)} fusion(f32[16,8,128,128]{2,3,1,0:T(8,128)} %get-tuple-element.325, pred[]{:T(512)S(6)} %compare.5, bf16[16,2,8,128,128]{4,2,3,1,0:T(8,128)(2,1)} %fusion.36, bf16[16,2,128,128]{3,2,1,0:T(8,128)(2,1)S(1)} %copy.100), kind=kOutput, calls=%fused_computation.5.clone.1 | convolution fusion | flops 1077936128 | bytes 26214400 | tf_op jit(solution)/shard_map/while/body/eval_jaxpr/ipab,ipnbc->inac/dot_general | solution.py:39
  247.0 7.2 %gather_fusion = bf16[32,3,128,128]{3,2,1,0:T(8,128)(2,1)} fusion(bf16[128,3,128,128]{3,2,1,0:T(8,128)(2,1)} %get-tuple-element.344, s32[1024]{0:T(1024)S(1)} %pad_clamp_fusion.4), kind=kCustom, calls=%fused_computation.1.clone.clone.1 | custom fusion | bytes 6291584 | tf_op jit(solution)/shard_map/while/body/eval_jaxpr/jit(_take)/gather | solution.py:33
  255.2 7.9 %fusion.36 = bf16[16,2,8,128,128]{4,2,3,1,0:T(8,128)(2,1)} fusion(bf16[16,2,3,128,128]{4,3,2,1,0:T(8,128)(2,1)} %bitcast.56, pred[16,2]{1,0:T(8,128)(4,1)S(1)} %copy.91, s32[16,8]{1,0:T(8,128)S(1)} %get-tuple-element.343, s32[16,2,3]{2,1,0:T(2,128)S(1)} %copy.93), kind=kOutput, calls=%fused_computation.9.clone.1 | convolution fusion | flops 26739456 | bytes 11535264 | tf_op jit(solution)/shard_map/while/body/eval_jaxpr/ipqn,ipqbc->ipnbc/dot_general | solution.py:36
  263.1 11.7 %bitcast_add_fusion.3 = f32[16,8,128,128]{2,3,1,0:T(8,128)} fusion(f32[16,8,128,128]{2,3,1,0:T(8,128)} %get-tuple-element.325, pred[]{:T(512)S(6)} %compare.5, bf16[16,2,8,128,128]{4,2,3,1,0:T(8,128)(2,1)} %fusion.36, bf16[16,2,128,128]{3,2,1,0:T(8,128)(2,1)S(1)} %copy.100), kind=kOutput, calls=%fused_computation.5.clone.1 | convolution fusion | flops 1077936128 | bytes 26214400 | tf_op jit(solution)/shard_map/while/body/eval_jaxpr/ipab,ipnbc->inac/dot_general | solution.py:39
  276.0 7.2 %gather_fusion = bf16[32,3,128,128]{3,2,1,0:T(8,128)(2,1)} fusion(bf16[128,3,128,128]{3,2,1,0:T(8,128)(2,1)} %get-tuple-element.344, s32[1024]{0:T(1024)S(1)} %pad_clamp_fusion.4), kind=kCustom, calls=%fused_computation.1.clone.clone.1 | custom fusion | bytes 6291584 | tf_op jit(solution)/shard_map/while/body/eval_jaxpr/jit(_take)/gather | solution.py:33
  284.2 7.9 %fusion.36 = bf16[16,2,8,128,128]{4,2,3,1,0:T(8,128)(2,1)} fusion(bf16[16,2,3,128,128]{4,3,2,1,0:T(8,128)(2,1)} %bitcast.56, pred[16,2]{1,0:T(8,128)(4,1)S(1)} %copy.91, s32[16,8]{1,0:T(8,128)S(1)} %get-tuple-element.343, s32[16,2,3]{2,1,0:T(2,128)S(1)} %copy.93), kind=kOutput, calls=%fused_computation.9.clone.1 | convolution fusion | flops 26739456 | bytes 11535264 | tf_op jit(solution)/shard_map/while/body/eval_jaxpr/ipqn,ipqbc->ipnbc/dot_general | solution.py:36
  292.1 11.7 %bitcast_add_fusion.3 = f32[16,8,128,128]{2,3,1,0:T(8,128)} fusion(f32[16,8,128,128]{2,3,1,0:T(8,128)} %get-tuple-element.325, pred[]{:T(512)S(6)} %compare.5, bf16[16,2,8,128,128]{4,2,3,1,0:T(8,128)(2,1)} %fusion.36, bf16[16,2,128,128]{3,2,1,0:T(8,128)(2,1)S(1)} %copy.100), kind=kOutput, calls=%fused_computation.5.clone.1 | convolution fusion | flops 1077936128 | bytes 26214400 | tf_op jit(solution)/shard_map/while/body/eval_jaxpr/ipab,ipnbc->inac/dot_general | solution.py:39
  306.5 7.2 %gather_fusion = bf16[32,3,128,128]{3,2,1,0:T(8,128)(2,1)} fusion(bf16[128,3,128,128]{3,2,1,0:T(8,128)(2,1)} %get-tuple-element.344, s32[1024]{0:T(1024)S(1)} %pad_clamp_fusion.4), kind=kCustom, calls=%fused_computation.1.clone.clone.1 | custom fusion | bytes 6291584 | tf_op jit(solution)/shard_map/while/body/eval_jaxpr/jit(_take)/gather | solution.py:33
  314.7 7.9 %fusion.36 = bf16[16,2,8,128,128]{4,2,3,1,0:T(8,128)(2,1)} fusion(bf16[16,2,3,128,128]{4,3,2,1,0:T(8,128)(2,1)} %bitcast.56, pred[16,2]{1,0:T(8,128)(4,1)S(1)} %copy.91, s32[16,8]{1,0:T(8,128)S(1)} %get-tuple-element.343, s32[16,2,3]{2,1,0:T(2,128)S(1)} %copy.93), kind=kOutput, calls=%fused_computation.9.clone.1 | convolution fusion | flops 26739456 | bytes 11535264 | tf_op jit(solution)/shard_map/while/body/eval_jaxpr/ipqn,ipqbc->ipnbc/dot_general | solution.py:36
  322.6 11.7 %bitcast_add_fusion.3 = f32[16,8,128,128]{2,3,1,0:T(8,128)} fusion(f32[16,8,128,128]{2,3,1,0:T(8,128)} %get-tuple-element.325, pred[]{:T(512)S(6)} %compare.5, bf16[16,2,8,128,128]{4,2,3,1,0:T(8,128)(2,1)} %fusion.36, bf16[16,2,128,128]{3,2,1,0:T(8,128)(2,1)S(1)} %copy.100), kind=kOutput, calls=%fused_computation.5.clone.1 | convolution fusion | flops 1077936128 | bytes 26214400 | tf_op jit(solution)/shard_map/while/body/eval_jaxpr/ipab,ipnbc->inac/dot_general | solution.py:39
  335.5 7.2 %gather_fusion = bf16[32,3,128,128]{3,2,1,0:T(8,128)(2,1)} fusion(bf16[128,3,128,128]{3,2,1,0:T(8,128)(2,1)} %get-tuple-element.344, s32[1024]{0:T(1024)S(1)} %pad_clamp_fusion.4), kind=kCustom, calls=%fused_computation.1.clone.clone.1 | custom fusion | bytes 6291584 | tf_op jit(solution)/shard_map/while/body/eval_jaxpr/jit(_take)/gather | solution.py:33
  343.7 7.9 %fusion.36 = bf16[16,2,8,128,128]{4,2,3,1,0:T(8,128)(2,1)} fusion(bf16[16,2,3,128,128]{4,3,2,1,0:T(8,128)(2,1)} %bitcast.56, pred[16,2]{1,0:T(8,128)(4,1)S(1)} %copy.91, s32[16,8]{1,0:T(8,128)S(1)} %get-tuple-element.343, s32[16,2,3]{2,1,0:T(2,128)S(1)} %copy.93), kind=kOutput, calls=%fused_computation.9.clone.1 | convolution fusion | flops 26739456 | bytes 11535264 | tf_op jit(solution)/shard_map/while/body/eval_jaxpr/ipqn,ipqbc->ipnbc/dot_general | solution.py:36
  351.6 11.7 %bitcast_add_fusion.3 = f32[16,8,128,128]{2,3,1,0:T(8,128)} fusion(f32[16,8,128,128]{2,3,1,0:T(8,128)} %get-tuple-element.325, pred[]{:T(512)S(6)} %compare.5, bf16[16,2,8,128,128]{4,2,3,1,0:T(8,128)(2,1)} %fusion.36, bf16[16,2,128,128]{3,2,1,0:T(8,128)(2,1)S(1)} %copy.100), kind=kOutput, calls=%fused_computation.5.clone.1 | convolution fusion | flops 1077936128 | bytes 26214400 | tf_op jit(solution)/shard_map/while/body/eval_jaxpr/ipab,ipnbc->inac/dot_general | solution.py:39
  365.3 7.2 %gather_fusion = bf16[32,3,128,128]{3,2,1,0:T(8,128)(2,1)} fusion(bf16[128,3,128,128]{3,2,1,0:T(8,128)(2,1)} %get-tuple-element.344, s32[1024]{0:T(1024)S(1)} %pad_clamp_fusion.4), kind=kCustom, calls=%fused_computation.1.clone.clone.1 | custom fusion | bytes 6291584 | tf_op jit(solution)/shard_map/while/body/eval_jaxpr/jit(_take)/gather | solution.py:33
  373.5 7.9 %fusion.36 = bf16[16,2,8,128,128]{4,2,3,1,0:T(8,128)(2,1)} fusion(bf16[16,2,3,128,128]{4,3,2,1,0:T(8,128)(2,1)} %bitcast.56, pred[16,2]{1,0:T(8,128)(4,1)S(1)} %copy.91, s32[16,8]{1,0:T(8,128)S(1)} %get-tuple-element.343, s32[16,2,3]{2,1,0:T(2,128)S(1)} %copy.93), kind=kOutput, calls=%fused_computation.9.clone.1 | convolution fusion | flops 26739456 | bytes 11535264 | tf_op jit(solution)/shard_map/while/body/eval_jaxpr/ipqn,ipqbc->ipnbc/dot_general | solution.py:36
  381.4 11.7 %bitcast_add_fusion.3 = f32[16,8,128,128]{2,3,1,0:T(8,128)} fusion(f32[16,8,128,128]{2,3,1,0:T(8,128)} %get-tuple-element.325, pred[]{:T(512)S(6)} %compare.5, bf16[16,2,8,128,128]{4,2,3,1,0:T(8,128)(2,1)} %fusion.36, bf16[16,2,128,128]{3,2,1,0:T(8,128)(2,1)S(1)} %copy.100), kind=kOutput, calls=%fused_computation.5.clone.1 | convolution fusion | flops 1077936128 | bytes 26214400 | tf_op jit(solution)/shard_map/while/body/eval_jaxpr/ipab,ipnbc->inac/dot_general | solution.py:39
  394.3 7.2 %gather_fusion = bf16[32,3,128,128]{3,2,1,0:T(8,128)(2,1)} fusion(bf16[128,3,128,128]{3,2,1,0:T(8,128)(2,1)} %get-tuple-element.344, s32[1024]{0:T(1024)S(1)} %pad_clamp_fusion.4), kind=kCustom, calls=%fused_computation.1.clone.clone.1 | custom fusion | bytes 6291584 | tf_op jit(solution)/shard_map/while/body/eval_jaxpr/jit(_take)/gather | solution.py:33
  402.5 7.9 %fusion.36 = bf16[16,2,8,128,128]{4,2,3,1,0:T(8,128)(2,1)} fusion(bf16[16,2,3,128,128]{4,3,2,1,0:T(8,128)(2,1)} %bitcast.56, pred[16,2]{1,0:T(8,128)(4,1)S(1)} %copy.91, s32[16,8]{1,0:T(8,128)S(1)} %get-tuple-element.343, s32[16,2,3]{2,1,0:T(2,128)S(1)} %copy.93), kind=kOutput, calls=%fused_computation.9.clone.1 | convolution fusion | flops 26739456 | bytes 11535264 | tf_op jit(solution)/shard_map/while/body/eval_jaxpr/ipqn,ipqbc->ipnbc/dot_general | solution.py:36
  410.4 11.7 %bitcast_add_fusion.3 = f32[16,8,128,128]{2,3,1,0:T(8,128)} fusion(f32[16,8,128,128]{2,3,1,0:T(8,128)} %get-tuple-element.325, pred[]{:T(512)S(6)} %compare.5, bf16[16,2,8,128,128]{4,2,3,1,0:T(8,128)(2,1)} %fusion.36, bf16[16,2,128,128]{3,2,1,0:T(8,128)(2,1)S(1)} %copy.100), kind=kOutput, calls=%fused_computation.5.clone.1 | convolution fusion | flops 1077936128 | bytes 26214400 | tf_op jit(solution)/shard_map/while/body/eval_jaxpr/ipab,ipnbc->inac/dot_general | solution.py:39
  433.2 7.9 %fusion.36 = bf16[16,2,8,128,128]{4,2,3,1,0:T(8,128)(2,1)} fusion(bf16[16,2,3,128,128]{4,3,2,1,0:T(8,128)(2,1)} %bitcast.56, pred[16,2]{1,0:T(8,128)(4,1)S(1)} %copy.91, s32[16,8]{1,0:T(8,128)S(1)} %get-tuple-element.343, s32[16,2,3]{2,1,0:T(2,128)S(1)} %copy.93), kind=kOutput, calls=%fused_computation.9.clone.1 | convolution fusion | flops 26739456 | bytes 11535264 | tf_op jit(solution)/shard_map/while/body/eval_jaxpr/ipqn,ipqbc->ipnbc/dot_general | solution.py:36
  441.2 11.7 %bitcast_add_fusion.3 = f32[16,8,128,128]{2,3,1,0:T(8,128)} fusion(f32[16,8,128,128]{2,3,1,0:T(8,128)} %get-tuple-element.325, pred[]{:T(512)S(6)} %compare.5, bf16[16,2,8,128,128]{4,2,3,1,0:T(8,128)(2,1)} %fusion.36, bf16[16,2,128,128]{3,2,1,0:T(8,128)(2,1)S(1)} %copy.100), kind=kOutput, calls=%fused_computation.5.clone.1 | convolution fusion | flops 1077936128 | bytes 26214400 | tf_op jit(solution)/shard_map/while/body/eval_jaxpr/ipab,ipnbc->inac/dot_general | solution.py:39
  462.2 7.9 %fusion.36 = bf16[16,2,8,128,128]{4,2,3,1,0:T(8,128)(2,1)} fusion(bf16[16,2,3,128,128]{4,3,2,1,0:T(8,128)(2,1)} %bitcast.56, pred[16,2]{1,0:T(8,128)(4,1)S(1)} %copy.91, s32[16,8]{1,0:T(8,128)S(1)} %get-tuple-element.343, s32[16,2,3]{2,1,0:T(2,128)S(1)} %copy.93), kind=kOutput, calls=%fused_computation.9.clone.1 | convolution fusion | flops 26739456 | bytes 11535264 | tf_op jit(solution)/shard_map/while/body/eval_jaxpr/ipqn,ipqbc->ipnbc/dot_general | solution.py:36
  470.2 11.7 %bitcast_add_fusion.3 = f32[16,8,128,128]{2,3,1,0:T(8,128)} fusion(f32[16,8,128,128]{2,3,1,0:T(8,128)} %get-tuple-element.325, pred[]{:T(512)S(6)} %compare.5, bf16[16,2,8,128,128]{4,2,3,1,0:T(8,128)(2,1)} %fusion.36, bf16[16,2,128,128]{3,2,1,0:T(8,128)(2,1)S(1)} %copy.100), kind=kOutput, calls=%fused_computation.5.clone.1 | convolution fusion | flops 1077936128 | bytes 26214400 | tf_op jit(solution)/shard_map/while/body/eval_jaxpr/ipab,ipnbc->inac/dot_general | solution.py:39
  484.8 7.2 %gather_fusion = bf16[32,3,128,128]{3,2,1,0:T(8,128)(2,1)} fusion(bf16[128,3,128,128]{3,2,1,0:T(8,128)(2,1)} %get-tuple-element.344, s32[1024]{0:T(1024)S(1)} %pad_clamp_fusion.4), kind=kCustom, calls=%fused_computation.1.clone.clone.1 | custom fusion | bytes 6291584 | tf_op jit(solution)/shard_map/while/body/eval_jaxpr/jit(_take)/gather | solution.py:33
  493.0 7.9 %fusion.36 = bf16[16,2,8,128,128]{4,2,3,1,0:T(8,128)(2,1)} fusion(bf16[16,2,3,128,128]{4,3,2,1,0:T(8,128)(2,1)} %bitcast.56, pred[16,2]{1,0:T(8,128)(4,1)S(1)} %copy.91, s32[16,8]{1,0:T(8,128)S(1)} %get-tuple-element.343, s32[16,2,3]{2,1,0:T(2,128)S(1)} %copy.93), kind=kOutput, calls=%fused_computation.9.clone.1 | convolution fusion | flops 26739456 | bytes 11535264 | tf_op jit(solution)/shard_map/while/body/eval_jaxpr/ipqn,ipqbc->ipnbc/dot_general | solution.py:36
  500.9 11.7 %bitcast_add_fusion.3 = f32[16,8,128,128]{2,3,1,0:T(8,128)} fusion(f32[16,8,128,128]{2,3,1,0:T(8,128)} %get-tuple-element.325, pred[]{:T(512)S(6)} %compare.5, bf16[16,2,8,128,128]{4,2,3,1,0:T(8,128)(2,1)} %fusion.36, bf16[16,2,128,128]{3,2,1,0:T(8,128)(2,1)S(1)} %copy.100), kind=kOutput, calls=%fused_computation.5.clone.1 | convolution fusion | flops 1077936128 | bytes 26214400 | tf_op jit(solution)/shard_map/while/body/eval_jaxpr/ipab,ipnbc->inac/dot_general | solution.py:39
  513.8 7.2 %gather_fusion = bf16[32,3,128,128]{3,2,1,0:T(8,128)(2,1)} fusion(bf16[128,3,128,128]{3,2,1,0:T(8,128)(2,1)} %get-tuple-element.344, s32[1024]{0:T(1024)S(1)} %pad_clamp_fusion.4), kind=kCustom, calls=%fused_computation.1.clone.clone.1 | custom fusion | bytes 6291584 | tf_op jit(solution)/shard_map/while/body/eval_jaxpr/jit(_take)/gather | solution.py:33
  522.0 7.9 %fusion.36 = bf16[16,2,8,128,128]{4,2,3,1,0:T(8,128)(2,1)} fusion(bf16[16,2,3,128,128]{4,3,2,1,0:T(8,128)(2,1)} %bitcast.56, pred[16,2]{1,0:T(8,128)(4,1)S(1)} %copy.91, s32[16,8]{1,0:T(8,128)S(1)} %get-tuple-element.343, s32[16,2,3]{2,1,0:T(2,128)S(1)} %copy.93), kind=kOutput, calls=%fused_computation.9.clone.1 | convolution fusion | flops 26739456 | bytes 11535264 | tf_op jit(solution)/shard_map/while/body/eval_jaxpr/ipqn,ipqbc->ipnbc/dot_general | solution.py:36
  529.9 11.7 %bitcast_add_fusion.3 = f32[16,8,128,128]{2,3,1,0:T(8,128)} fusion(f32[16,8,128,128]{2,3,1,0:T(8,128)} %get-tuple-element.325, pred[]{:T(512)S(6)} %compare.5, bf16[16,2,8,128,128]{4,2,3,1,0:T(8,128)(2,1)} %fusion.36, bf16[16,2,128,128]{3,2,1,0:T(8,128)(2,1)S(1)} %copy.100), kind=kOutput, calls=%fused_computation.5.clone.1 | convolution fusion | flops 1077936128 | bytes 26214400 | tf_op jit(solution)/shard_map/while/body/eval_jaxpr/ipab,ipnbc->inac/dot_general | solution.py:39
  552.5 7.9 %fusion.36 = bf16[16,2,8,128,128]{4,2,3,1,0:T(8,128)(2,1)} fusion(bf16[16,2,3,128,128]{4,3,2,1,0:T(8,128)(2,1)} %bitcast.56, pred[16,2]{1,0:T(8,128)(4,1)S(1)} %copy.91, s32[16,8]{1,0:T(8,128)S(1)} %get-tuple-element.343, s32[16,2,3]{2,1,0:T(2,128)S(1)} %copy.93), kind=kOutput, calls=%fused_computation.9.clone.1 | convolution fusion | flops 26739456 | bytes 11535264 | tf_op jit(solution)/shard_map/while/body/eval_jaxpr/ipqn,ipqbc->ipnbc/dot_general | solution.py:36
  560.4 11.7 %bitcast_add_fusion.3 = f32[16,8,128,128]{2,3,1,0:T(8,128)} fusion(f32[16,8,128,128]{2,3,1,0:T(8,128)} %get-tuple-element.325, pred[]{:T(512)S(6)} %compare.5, bf16[16,2,8,128,128]{4,2,3,1,0:T(8,128)(2,1)} %fusion.36, bf16[16,2,128,128]{3,2,1,0:T(8,128)(2,1)S(1)} %copy.100), kind=kOutput, calls=%fused_computation.5.clone.1 | convolution fusion | flops 1077936128 | bytes 26214400 | tf_op jit(solution)/shard_map/while/body/eval_jaxpr/ipab,ipnbc->inac/dot_general | solution.py:39
  573.3 7.2 %gather_fusion = bf16[32,3,128,128]{3,2,1,0:T(8,128)(2,1)} fusion(bf16[128,3,128,128]{3,2,1,0:T(8,128)(2,1)} %get-tuple-element.344, s32[1024]{0:T(1024)S(1)} %pad_clamp_fusion.4), kind=kCustom, calls=%fused_computation.1.clone.clone.1 | custom fusion | bytes 6291584 | tf_op jit(solution)/shard_map/while/body/eval_jaxpr/jit(_take)/gather | solution.py:33
  581.5 7.9 %fusion.36 = bf16[16,2,8,128,128]{4,2,3,1,0:T(8,128)(2,1)} fusion(bf16[16,2,3,128,128]{4,3,2,1,0:T(8,128)(2,1)} %bitcast.56, pred[16,2]{1,0:T(8,128)(4,1)S(1)} %copy.91, s32[16,8]{1,0:T(8,128)S(1)} %get-tuple-element.343, s32[16,2,3]{2,1,0:T(2,128)S(1)} %copy.93), kind=kOutput, calls=%fused_computation.9.clone.1 | convolution fusion | flops 26739456 | bytes 11535264 | tf_op jit(solution)/shard_map/while/body/eval_jaxpr/ipqn,ipqbc->ipnbc/dot_general | solution.py:36
  589.4 11.7 %bitcast_add_fusion.3 = f32[16,8,128,128]{2,3,1,0:T(8,128)} fusion(f32[16,8,128,128]{2,3,1,0:T(8,128)} %get-tuple-element.325, pred[]{:T(512)S(6)} %compare.5, bf16[16,2,8,128,128]{4,2,3,1,0:T(8,128)(2,1)} %fusion.36, bf16[16,2,128,128]{3,2,1,0:T(8,128)(2,1)S(1)} %copy.100), kind=kOutput, calls=%fused_computation.5.clone.1 | convolution fusion | flops 1077936128 | bytes 26214400 | tf_op jit(solution)/shard_map/while/body/eval_jaxpr/ipab,ipnbc->inac/dot_general | solution.py:39
  609.6 8.0 %fusion.16 = bf16[16,2,8,128,128]{4,2,3,1,0:T(8,128)(2,1)} fusion(bf16[16,2,3,128,128]{4,3,2,1,0:T(8,128)(2,1)} %bitcast.59, pred[16,2]{1,0:T(8,128)(4,1)S(1)} %copy.50, s32[16,8]{1,0:T(8,128)S(1)} %get-tuple-element.359, s32[16,2,3]{2,1,0:T(2,128)S(1)} %copy.54), kind=kOutput, calls=%fused_computation.27 | convolution fusion | flops 26739456 | bytes 11535264 | tf_op jit(solution)/shard_map/ipqn,ipqbc->ipnbc/dot_general | solution.py:36
  617.6 10.5 %fusion.13 = bf16[16,8,128,128]{2,3,1,0:T(8,128)(2,1)} fusion(f32[16,8,128,128]{2,3,1,0:T(8,128)} %get-tuple-element.208, bf16[16,2,8,128,128]{4,2,3,1,0:T(8,128)(2,1)} %fusion.16, bf16[16,2,128,128]{3,2,1,0:T(8,128)(2,1)S(1)} %get-tuple-element.210), kind=kOutput, calls=%fused_computation.23 | convolution fusion | flops 1077936128 | bytes 22020096 | tf_op jit(solution)/shard_map/ipab,ipnbc->inac/dot_general | solution.py:39
  642.4 58.3 %all_to_all.5 = bf16[128,128,128]{2,1,0:T(8,128)(2,1)S(1)} all-to-all(bf16[128,128,128]{2,1,0:T(8,128)(2,1)S(1)} %broadcast_select_fusion.1), channel_id=1, replica_groups=mesh['row'=8,'col'=16] {'row','col'}, dimensions={0} | all-to-all | bytes 8388608 | tf_op jit(solution)/shard_map/all_to_all | solution.py:62
  (271 shorter events, 95.0 us)
Async XLA Ops:
  6.5 150.2 %all-gather.3.cloned.1.call-start = ((), (), s32[]{:S(2)}) async-start(), calls=%async_computation.1 | async-start | bytes 14155776 | tf_op jit(solution)/shard_map/all_gather | solution.py:22
  156.8 27.5 %collective-permute-start = (bf16[16,2,128,128]{3,2,1,0:T(8,128)(2,1)S(1)}, bf16[16,2,128,128]{3,2,1,0:T(8,128)(2,1)S(1)}, u32[]{:S(2)}, u32[]{:S(2)}) collective-permute-start(bf16[16,2,128,128]{3,2,1,0:T(8,128)(2,1)S(1)} %copy.100), channel_id=1, source_target_pairs={{0,1},{1,2},{2,3},{3,4},{4,5},{5,6},{6,7},{7,8},{8,9},{9,10},{10,1... | collective-permute-start | bytes 3145736 | tf_op jit(solution)/shard_map/while/body/eval_jaxpr/ppermute | solution.py:11
  158.5 25.9 %collective-permute-start.1 = (bf16[16,2]{0,1:T(2,128)(2,1)S(1)}, bf16[16,2]{0,1:T(2,128)(2,1)S(1)}, u32[]{:S(2)}, u32[]{:S(2)}) collective-permute-start(bf16[16,2]{0,1:T(2,128)(2,1)S(1)} %copy.101), channel_id=1, source_target_pairs={{0,1},{1,2},{2,3},{3,4},{4,5},{5,6},{6,7},{7,8},{8,9},{9,10},{10,1... | collective-permute-start | bytes 200 | tf_op jit(solution)/shard_map/while/body/eval_jaxpr/ppermute | solution.py:11
  184.4 30.7 %collective-permute-start = (bf16[16,2,128,128]{3,2,1,0:T(8,128)(2,1)S(1)}, bf16[16,2,128,128]{3,2,1,0:T(8,128)(2,1)S(1)}, u32[]{:S(2)}, u32[]{:S(2)}) collective-permute-start(bf16[16,2,128,128]{3,2,1,0:T(8,128)(2,1)S(1)} %copy.100), channel_id=1, source_target_pairs={{0,1},{1,2},{2,3},{3,4},{4,5},{5,6},{6,7},{7,8},{8,9},{9,10},{10,1... | collective-permute-start | bytes 3145736 | tf_op jit(solution)/shard_map/while/body/eval_jaxpr/ppermute | solution.py:11
  186.9 28.2 %collective-permute-start.1 = (bf16[16,2]{0,1:T(2,128)(2,1)S(1)}, bf16[16,2]{0,1:T(2,128)(2,1)S(1)}, u32[]{:S(2)}, u32[]{:S(2)}) collective-permute-start(bf16[16,2]{0,1:T(2,128)(2,1)S(1)} %copy.101), channel_id=1, source_target_pairs={{0,1},{1,2},{2,3},{3,4},{4,5},{5,6},{6,7},{7,8},{8,9},{9,10},{10,1... | collective-permute-start | bytes 200 | tf_op jit(solution)/shard_map/while/body/eval_jaxpr/ppermute | solution.py:11
  215.2 28.9 %collective-permute-start = (bf16[16,2,128,128]{3,2,1,0:T(8,128)(2,1)S(1)}, bf16[16,2,128,128]{3,2,1,0:T(8,128)(2,1)S(1)}, u32[]{:S(2)}, u32[]{:S(2)}) collective-permute-start(bf16[16,2,128,128]{3,2,1,0:T(8,128)(2,1)S(1)} %copy.100), channel_id=1, source_target_pairs={{0,1},{1,2},{2,3},{3,4},{4,5},{5,6},{6,7},{7,8},{8,9},{9,10},{10,1... | collective-permute-start | bytes 3145736 | tf_op jit(solution)/shard_map/while/body/eval_jaxpr/ppermute | solution.py:11
  215.9 28.2 %collective-permute-start.1 = (bf16[16,2]{0,1:T(2,128)(2,1)S(1)}, bf16[16,2]{0,1:T(2,128)(2,1)S(1)}, u32[]{:S(2)}, u32[]{:S(2)}) collective-permute-start(bf16[16,2]{0,1:T(2,128)(2,1)S(1)} %copy.101), channel_id=1, source_target_pairs={{0,1},{1,2},{2,3},{3,4},{4,5},{5,6},{6,7},{7,8},{8,9},{9,10},{10,1... | collective-permute-start | bytes 200 | tf_op jit(solution)/shard_map/while/body/eval_jaxpr/ppermute | solution.py:11
  244.2 30.7 %collective-permute-start = (bf16[16,2,128,128]{3,2,1,0:T(8,128)(2,1)S(1)}, bf16[16,2,128,128]{3,2,1,0:T(8,128)(2,1)S(1)}, u32[]{:S(2)}, u32[]{:S(2)}) collective-permute-start(bf16[16,2,128,128]{3,2,1,0:T(8,128)(2,1)S(1)} %copy.100), channel_id=1, source_target_pairs={{0,1},{1,2},{2,3},{3,4},{4,5},{5,6},{6,7},{7,8},{8,9},{9,10},{10,1... | collective-permute-start | bytes 3145736 | tf_op jit(solution)/shard_map/while/body/eval_jaxpr/ppermute | solution.py:11
  246.6 28.2 %collective-permute-start.1 = (bf16[16,2]{0,1:T(2,128)(2,1)S(1)}, bf16[16,2]{0,1:T(2,128)(2,1)S(1)}, u32[]{:S(2)}, u32[]{:S(2)}) collective-permute-start(bf16[16,2]{0,1:T(2,128)(2,1)S(1)} %copy.101), channel_id=1, source_target_pairs={{0,1},{1,2},{2,3},{3,4},{4,5},{5,6},{6,7},{7,8},{8,9},{9,10},{10,1... | collective-permute-start | bytes 200 | tf_op jit(solution)/shard_map/while/body/eval_jaxpr/ppermute | solution.py:11
  274.9 28.9 %collective-permute-start = (bf16[16,2,128,128]{3,2,1,0:T(8,128)(2,1)S(1)}, bf16[16,2,128,128]{3,2,1,0:T(8,128)(2,1)S(1)}, u32[]{:S(2)}, u32[]{:S(2)}) collective-permute-start(bf16[16,2,128,128]{3,2,1,0:T(8,128)(2,1)S(1)} %copy.100), channel_id=1, source_target_pairs={{0,1},{1,2},{2,3},{3,4},{4,5},{5,6},{6,7},{7,8},{8,9},{9,10},{10,1... | collective-permute-start | bytes 3145736 | tf_op jit(solution)/shard_map/while/body/eval_jaxpr/ppermute | solution.py:11
  275.6 28.2 %collective-permute-start.1 = (bf16[16,2]{0,1:T(2,128)(2,1)S(1)}, bf16[16,2]{0,1:T(2,128)(2,1)S(1)}, u32[]{:S(2)}, u32[]{:S(2)}) collective-permute-start(bf16[16,2]{0,1:T(2,128)(2,1)S(1)} %copy.101), channel_id=1, source_target_pairs={{0,1},{1,2},{2,3},{3,4},{4,5},{5,6},{6,7},{7,8},{8,9},{9,10},{10,1... | collective-permute-start | bytes 200 | tf_op jit(solution)/shard_map/while/body/eval_jaxpr/ppermute | solution.py:11
  303.9 30.4 %collective-permute-start = (bf16[16,2,128,128]{3,2,1,0:T(8,128)(2,1)S(1)}, bf16[16,2,128,128]{3,2,1,0:T(8,128)(2,1)S(1)}, u32[]{:S(2)}, u32[]{:S(2)}) collective-permute-start(bf16[16,2,128,128]{3,2,1,0:T(8,128)(2,1)S(1)} %copy.100), channel_id=1, source_target_pairs={{0,1},{1,2},{2,3},{3,4},{4,5},{5,6},{6,7},{7,8},{8,9},{9,10},{10,1... | collective-permute-start | bytes 3145736 | tf_op jit(solution)/shard_map/while/body/eval_jaxpr/ppermute | solution.py:11
  306.1 28.2 %collective-permute-start.1 = (bf16[16,2]{0,1:T(2,128)(2,1)S(1)}, bf16[16,2]{0,1:T(2,128)(2,1)S(1)}, u32[]{:S(2)}, u32[]{:S(2)}) collective-permute-start(bf16[16,2]{0,1:T(2,128)(2,1)S(1)} %copy.101), channel_id=1, source_target_pairs={{0,1},{1,2},{2,3},{3,4},{4,5},{5,6},{6,7},{7,8},{8,9},{9,10},{10,1... | collective-permute-start | bytes 200 | tf_op jit(solution)/shard_map/while/body/eval_jaxpr/ppermute | solution.py:11
  334.4 28.9 %collective-permute-start = (bf16[16,2,128,128]{3,2,1,0:T(8,128)(2,1)S(1)}, bf16[16,2,128,128]{3,2,1,0:T(8,128)(2,1)S(1)}, u32[]{:S(2)}, u32[]{:S(2)}) collective-permute-start(bf16[16,2,128,128]{3,2,1,0:T(8,128)(2,1)S(1)} %copy.100), channel_id=1, source_target_pairs={{0,1},{1,2},{2,3},{3,4},{4,5},{5,6},{6,7},{7,8},{8,9},{9,10},{10,1... | collective-permute-start | bytes 3145736 | tf_op jit(solution)/shard_map/while/body/eval_jaxpr/ppermute | solution.py:11
  335.1 28.2 %collective-permute-start.1 = (bf16[16,2]{0,1:T(2,128)(2,1)S(1)}, bf16[16,2]{0,1:T(2,128)(2,1)S(1)}, u32[]{:S(2)}, u32[]{:S(2)}) collective-permute-start(bf16[16,2]{0,1:T(2,128)(2,1)S(1)} %copy.101), channel_id=1, source_target_pairs={{0,1},{1,2},{2,3},{3,4},{4,5},{5,6},{6,7},{7,8},{8,9},{9,10},{10,1... | collective-permute-start | bytes 200 | tf_op jit(solution)/shard_map/while/body/eval_jaxpr/ppermute | solution.py:11
  363.4 29.8 %collective-permute-start = (bf16[16,2,128,128]{3,2,1,0:T(8,128)(2,1)S(1)}, bf16[16,2,128,128]{3,2,1,0:T(8,128)(2,1)S(1)}, u32[]{:S(2)}, u32[]{:S(2)}) collective-permute-start(bf16[16,2,128,128]{3,2,1,0:T(8,128)(2,1)S(1)} %copy.100), channel_id=1, source_target_pairs={{0,1},{1,2},{2,3},{3,4},{4,5},{5,6},{6,7},{7,8},{8,9},{9,10},{10,1... | collective-permute-start | bytes 3145736 | tf_op jit(solution)/shard_map/while/body/eval_jaxpr/ppermute | solution.py:11
  364.9 28.2 %collective-permute-start.1 = (bf16[16,2]{0,1:T(2,128)(2,1)S(1)}, bf16[16,2]{0,1:T(2,128)(2,1)S(1)}, u32[]{:S(2)}, u32[]{:S(2)}) collective-permute-start(bf16[16,2]{0,1:T(2,128)(2,1)S(1)} %copy.101), channel_id=1, source_target_pairs={{0,1},{1,2},{2,3},{3,4},{4,5},{5,6},{6,7},{7,8},{8,9},{9,10},{10,1... | collective-permute-start | bytes 200 | tf_op jit(solution)/shard_map/while/body/eval_jaxpr/ppermute | solution.py:11
  393.2 28.9 %collective-permute-start = (bf16[16,2,128,128]{3,2,1,0:T(8,128)(2,1)S(1)}, bf16[16,2,128,128]{3,2,1,0:T(8,128)(2,1)S(1)}, u32[]{:S(2)}, u32[]{:S(2)}) collective-permute-start(bf16[16,2,128,128]{3,2,1,0:T(8,128)(2,1)S(1)} %copy.100), channel_id=1, source_target_pairs={{0,1},{1,2},{2,3},{3,4},{4,5},{5,6},{6,7},{7,8},{8,9},{9,10},{10,1... | collective-permute-start | bytes 3145736 | tf_op jit(solution)/shard_map/while/body/eval_jaxpr/ppermute | solution.py:11
  393.9 28.2 %collective-permute-start.1 = (bf16[16,2]{0,1:T(2,128)(2,1)S(1)}, bf16[16,2]{0,1:T(2,128)(2,1)S(1)}, u32[]{:S(2)}, u32[]{:S(2)}) collective-permute-start(bf16[16,2]{0,1:T(2,128)(2,1)S(1)} %copy.101), channel_id=1, source_target_pairs={{0,1},{1,2},{2,3},{3,4},{4,5},{5,6},{6,7},{7,8},{8,9},{9,10},{10,1... | collective-permute-start | bytes 200 | tf_op jit(solution)/shard_map/while/body/eval_jaxpr/ppermute | solution.py:11
  422.2 30.7 %collective-permute-start = (bf16[16,2,128,128]{3,2,1,0:T(8,128)(2,1)S(1)}, bf16[16,2,128,128]{3,2,1,0:T(8,128)(2,1)S(1)}, u32[]{:S(2)}, u32[]{:S(2)}) collective-permute-start(bf16[16,2,128,128]{3,2,1,0:T(8,128)(2,1)S(1)} %copy.100), channel_id=1, source_target_pairs={{0,1},{1,2},{2,3},{3,4},{4,5},{5,6},{6,7},{7,8},{8,9},{9,10},{10,1... | collective-permute-start | bytes 3145736 | tf_op jit(solution)/shard_map/while/body/eval_jaxpr/ppermute | solution.py:11
  424.7 28.2 %collective-permute-start.1 = (bf16[16,2]{0,1:T(2,128)(2,1)S(1)}, bf16[16,2]{0,1:T(2,128)(2,1)S(1)}, u32[]{:S(2)}, u32[]{:S(2)}) collective-permute-start(bf16[16,2]{0,1:T(2,128)(2,1)S(1)} %copy.101), channel_id=1, source_target_pairs={{0,1},{1,2},{2,3},{3,4},{4,5},{5,6},{6,7},{7,8},{8,9},{9,10},{10,1... | collective-permute-start | bytes 200 | tf_op jit(solution)/shard_map/while/body/eval_jaxpr/ppermute | solution.py:11
  453.0 28.9 %collective-permute-start = (bf16[16,2,128,128]{3,2,1,0:T(8,128)(2,1)S(1)}, bf16[16,2,128,128]{3,2,1,0:T(8,128)(2,1)S(1)}, u32[]{:S(2)}, u32[]{:S(2)}) collective-permute-start(bf16[16,2,128,128]{3,2,1,0:T(8,128)(2,1)S(1)} %copy.100), channel_id=1, source_target_pairs={{0,1},{1,2},{2,3},{3,4},{4,5},{5,6},{6,7},{7,8},{8,9},{9,10},{10,1... | collective-permute-start | bytes 3145736 | tf_op jit(solution)/shard_map/while/body/eval_jaxpr/ppermute | solution.py:11
  453.7 28.2 %collective-permute-start.1 = (bf16[16,2]{0,1:T(2,128)(2,1)S(1)}, bf16[16,2]{0,1:T(2,128)(2,1)S(1)}, u32[]{:S(2)}, u32[]{:S(2)}) collective-permute-start(bf16[16,2]{0,1:T(2,128)(2,1)S(1)} %copy.101), channel_id=1, source_target_pairs={{0,1},{1,2},{2,3},{3,4},{4,5},{5,6},{6,7},{7,8},{8,9},{9,10},{10,1... | collective-permute-start | bytes 200 | tf_op jit(solution)/shard_map/while/body/eval_jaxpr/ppermute | solution.py:11
  482.0 30.7 %collective-permute-start = (bf16[16,2,128,128]{3,2,1,0:T(8,128)(2,1)S(1)}, bf16[16,2,128,128]{3,2,1,0:T(8,128)(2,1)S(1)}, u32[]{:S(2)}, u32[]{:S(2)}) collective-permute-start(bf16[16,2,128,128]{3,2,1,0:T(8,128)(2,1)S(1)} %copy.100), channel_id=1, source_target_pairs={{0,1},{1,2},{2,3},{3,4},{4,5},{5,6},{6,7},{7,8},{8,9},{9,10},{10,1... | collective-permute-start | bytes 3145736 | tf_op jit(solution)/shard_map/while/body/eval_jaxpr/ppermute | solution.py:11
  484.4 28.2 %collective-permute-start.1 = (bf16[16,2]{0,1:T(2,128)(2,1)S(1)}, bf16[16,2]{0,1:T(2,128)(2,1)S(1)}, u32[]{:S(2)}, u32[]{:S(2)}) collective-permute-start(bf16[16,2]{0,1:T(2,128)(2,1)S(1)} %copy.101), channel_id=1, source_target_pairs={{0,1},{1,2},{2,3},{3,4},{4,5},{5,6},{6,7},{7,8},{8,9},{9,10},{10,1... | collective-permute-start | bytes 200 | tf_op jit(solution)/shard_map/while/body/eval_jaxpr/ppermute | solution.py:11
  512.7 28.9 %collective-permute-start = (bf16[16,2,128,128]{3,2,1,0:T(8,128)(2,1)S(1)}, bf16[16,2,128,128]{3,2,1,0:T(8,128)(2,1)S(1)}, u32[]{:S(2)}, u32[]{:S(2)}) collective-permute-start(bf16[16,2,128,128]{3,2,1,0:T(8,128)(2,1)S(1)} %copy.100), channel_id=1, source_target_pairs={{0,1},{1,2},{2,3},{3,4},{4,5},{5,6},{6,7},{7,8},{8,9},{9,10},{10,1... | collective-permute-start | bytes 3145736 | tf_op jit(solution)/shard_map/while/body/eval_jaxpr/ppermute | solution.py:11
  513.4 28.2 %collective-permute-start.1 = (bf16[16,2]{0,1:T(2,128)(2,1)S(1)}, bf16[16,2]{0,1:T(2,128)(2,1)S(1)}, u32[]{:S(2)}, u32[]{:S(2)}) collective-permute-start(bf16[16,2]{0,1:T(2,128)(2,1)S(1)} %copy.101), channel_id=1, source_target_pairs={{0,1},{1,2},{2,3},{3,4},{4,5},{5,6},{6,7},{7,8},{8,9},{9,10},{10,1... | collective-permute-start | bytes 200 | tf_op jit(solution)/shard_map/while/body/eval_jaxpr/ppermute | solution.py:11
  541.7 30.4 %collective-permute-start = (bf16[16,2,128,128]{3,2,1,0:T(8,128)(2,1)S(1)}, bf16[16,2,128,128]{3,2,1,0:T(8,128)(2,1)S(1)}, u32[]{:S(2)}, u32[]{:S(2)}) collective-permute-start(bf16[16,2,128,128]{3,2,1,0:T(8,128)(2,1)S(1)} %copy.100), channel_id=1, source_target_pairs={{0,1},{1,2},{2,3},{3,4},{4,5},{5,6},{6,7},{7,8},{8,9},{9,10},{10,1... | collective-permute-start | bytes 3145736 | tf_op jit(solution)/shard_map/while/body/eval_jaxpr/ppermute | solution.py:11
  543.9 28.2 %collective-permute-start.1 = (bf16[16,2]{0,1:T(2,128)(2,1)S(1)}, bf16[16,2]{0,1:T(2,128)(2,1)S(1)}, u32[]{:S(2)}, u32[]{:S(2)}) collective-permute-start(bf16[16,2]{0,1:T(2,128)(2,1)S(1)} %copy.101), channel_id=1, source_target_pairs={{0,1},{1,2},{2,3},{3,4},{4,5},{5,6},{6,7},{7,8},{8,9},{9,10},{10,1... | collective-permute-start | bytes 200 | tf_op jit(solution)/shard_map/while/body/eval_jaxpr/ppermute | solution.py:11
  572.2 28.9 %collective-permute-start = (bf16[16,2,128,128]{3,2,1,0:T(8,128)(2,1)S(1)}, bf16[16,2,128,128]{3,2,1,0:T(8,128)(2,1)S(1)}, u32[]{:S(2)}, u32[]{:S(2)}) collective-permute-start(bf16[16,2,128,128]{3,2,1,0:T(8,128)(2,1)S(1)} %copy.100), channel_id=1, source_target_pairs={{0,1},{1,2},{2,3},{3,4},{4,5},{5,6},{6,7},{7,8},{8,9},{9,10},{10,1... | collective-permute-start | bytes 3145736 | tf_op jit(solution)/shard_map/while/body/eval_jaxpr/ppermute | solution.py:11
  572.9 28.2 %collective-permute-start.1 = (bf16[16,2]{0,1:T(2,128)(2,1)S(1)}, bf16[16,2]{0,1:T(2,128)(2,1)S(1)}, u32[]{:S(2)}, u32[]{:S(2)}) collective-permute-start(bf16[16,2]{0,1:T(2,128)(2,1)S(1)} %copy.101), channel_id=1, source_target_pairs={{0,1},{1,2},{2,3},{3,4},{4,5},{5,6},{6,7},{7,8},{8,9},{9,10},{10,1... | collective-permute-start | bytes 200 | tf_op jit(solution)/shard_map/while/body/eval_jaxpr/ppermute | solution.py:11
Sparse Core Ops, SparseCore 0:
  9.6 147.0 all-gather.2
where the time goes:
time: 713 us; the launch traced here: 710 us
  matrix products  311 us (44%)
  local copies, waits for them, and re-layouts  152 us (21%)
  waiting for transfers between devices  124 us (17%)
  blocking collectives  80.1 us (11%)
  starting transfers between devices  23.3 us (3%)
  between operations  13.5 us (2%)
    dot_general x16, matrix products, accumulate(): jnp.einsum('ipab,ipnbc->inac', a_piece, selected, preferred_element_type=...  184 us
    dot_general x16, matrix products, accumulate(): jnp.einsum('ipqn,ipqbc->ipnbc', matches, b_chosen, preferred_element_type...  127 us
    all_gather x1, waiting for transfers between devices, on_device(): lax.all_gather(b_vals, 'row', axis=0, tiled=True)  124 us
    gather x16, local copies, waits for them, and re-layouts, accumulate(): b_chosen = jnp.take(b_whole, inner_rows, axis=0)  115 us
    all_to_all x1, blocking collectives, on_device(): lax.all_to_all(outgoing, ('row', 'col'), split_axis=0, concat_axis=0, til...  58.3 us
    ppermute x30, starting transfers between devices, from_behind(): lax.ppermute(shard, axis, [(i, (i + by) % length) for i in range(length)])  23.3 us
    all_gather x1, blocking collectives, on_device(): lax.all_gather(local_cols, 'row', axis=0, tiled=True)  21.8 us
  transfers between devices with their start and end apart: 31, of which 1 were waited for; matrix products, arithmetic and copies ran while one was open for 60% of the time, Pallas kernels for 0%

commit v1 on v0

v1 whole, which is shorter than its diff:
```python
import jax
import jax.numpy as jnp
from jax import lax
from jax.experimental import pallas as pl
from jax.experimental.pallas import tpu as pltpu
from jax.sharding import PartitionSpec as P

MESH = pl.DeviceIdType.MESH
N_ROW, N_COL = 8, 16
NX, NZ = 4, 4
BS = 128
SBD, PANEL = 16, 8
RB, NZS, NZBC, NZC = 16, 2, 3, 8
KEPT = RB * NZC
SLOTS = N_COL * NZS
ZERO = N_ROW * RB * NZBC
LIST_ROWS = SLOTS + 8
CODE = 512
HALF = RB // 2


def build_lists(aidx, bidx, ccol_ref, arep, brep, list_ref):
    for c in range(N_COL):
        arep[pl.ds(c, 1), :] = aidx[c, 2:3, :]
    for r in range(N_ROW):
        brep[pl.ds(2 * r, 2), :] = bidx[r, 0:2, :]
    lane_in = lax.broadcasted_iota(jnp.int32, (BS, BS), 0)
    lane_out = lax.broadcasted_iota(jnp.int32, (BS, BS), 1)
    offs = arep[...].astype(jnp.bfloat16)
    spread = []
    for s in range(NZS):
        pick = (lane_in == NZS * (lane_out // NZC) + s).astype(jnp.bfloat16)
        spread.append(jnp.dot(offs, pick, preferred_element_type=jnp.float32))
    aoff = jnp.concatenate(spread, axis=0).astype(jnp.int32)
    cols = jnp.concatenate([brep[...], brep[...]], axis=0)
    keep = jnp.broadcast_to(ccol_ref[0:1, :], (SLOTS, KEPT))
    turn = lax.broadcasted_iota(jnp.int32, (SLOTS, KEPT), 0)
    panel = turn % N_COL
    which = turn // N_COL
    found = jnp.zeros((SLOTS, KEPT), jnp.int32)
    for j in range(PANEL):
        here = aoff == j
        for q in range(NZBC):
            at = NZBC * j + q
            col = jnp.broadcast_to(cols[:, at : at + 1], (SLOTS, KEPT))
            found = jnp.where(here & (col == keep), panel * (PANEL * NZBC) + at + 1, found)
    hit = found > 0
    hits = hit.astype(jnp.float32).astype(jnp.bfloat16)
    row_id = lax.broadcasted_iota(jnp.int32, (SLOTS, SLOTS), 0)
    col_id = lax.broadcasted_iota(jnp.int32, (SLOTS, SLOTS), 1)
    below = (col_id < row_id).astype(jnp.float32).astype(jnp.bfloat16)
    rank = jnp.dot(below, hits, preferred_element_type=jnp.float32).astype(jnp.int32)
    rank = jnp.where(hit, rank, SLOTS)
    count = jnp.sum(hit.astype(jnp.int32), axis=0, keepdims=True)
    full = (panel * NZS + which) * CODE + found - 1
    for n in range(SLOTS):
        entry = jnp.sum(jnp.where(rank == n, full, 0), axis=0, keepdims=True)
        list_ref[pl.ds(n, 1), :] = jnp.where(count > n, entry, ZERO)
    list_ref[pl.ds(SLOTS, 8), :] = jnp.broadcast_to(count, (8, KEPT))


def gather_kernel(
    idx_ref, ccol_ref, a_ref, b_ref, a_all, b_all, list_ref,
    aidx, bidx, arep, brep, a_own, b_own, send, recv, isend, irecv, lsem,
):
    row, col = lax.axis_index("row"), lax.axis_index("col")
    yh, z = row // NZ, row % NZ
    x, yl, core = col // 4, (col // 2) % 2, col % 2

    def at_z(h, zz):
        return lax.rem(yh + h, 2) * NZ + lax.rem(zz + NZ, NZ)

    def at_x(h, xx):
        return lax.rem(xx + NX, NX) * 4 + lax.rem(yl + h, 2) * 2 + core

    twin = (row, col + 1 - 2 * core)
    barrier = pltpu.get_barrier_semaphore()
    row_peers = [(lax.rem(row + j, N_ROW), col) for j in range(1, N_ROW)]
    col_peers = [(row, lax.rem(col + j, N_COL)) for j in range(1, N_COL)]
    for peer in row_peers + col_peers:
        pl.semaphore_signal(barrier, inc=1, device_id=peer, device_id_type=MESH)
    pl.semaphore_wait(barrier, len(row_peers) + len(col_peers))

    started = []

    def put(src, dst, peer):
        n = len(started)
        copy = pltpu.make_async_remote_copy(
            src_ref=src, dst_ref=dst, send_sem=send.at[n], recv_sem=recv.at[n],
            device_id=peer, device_id_type=MESH,
        )
        copy.start()
        started.append(copy)
        return copy

    def piece(ref, slot, half):
        return ref.at[slot, pl.ds(half * HALF, HALF)]

    def b_src(h, half):
        return b_ref.at[pl.ds(half * HALF, HALF)] if h == 0 else piece(b_all, at_z(1, z), half)

    def a_src(h, half):
        return a_ref.at[pl.ds(half * HALF, HALF)] if h == 0 else piece(a_all, at_x(1, x), half)

    up, down = (at_z(0, z + 1), col), (at_z(0, z - 1), col)
    east, west = (row, at_x(0, x + 1)), (row, at_x(0, x - 1))

    def ring(src, whole, at, pos, h, plus, minus):
        slot = at(h, pos)
        p0 = put(src(h, 0), piece(whole, slot, 0), plus)
        m1 = put(src(h, 1), piece(whole, slot, 1), minus)
        p1 = put(src(h, 1), piece(whole, slot, 1), plus)
        m0 = put(src(h, 0), piece(whole, slot, 0), minus)
        return p0, m1, p1, m0

    def pass_on(whole, at, pos, h, step, half, peer):
        part = piece(whole, at(h, pos + step), half)
        return put(part, part, peer)

    def a_hand(h, step, half):
        part = piece(a_all, at_x(h, x + step), half)
        return put(part, part, twin)

    small = []
    for n, peer in enumerate(row_peers):
        copy = pltpu.make_async_remote_copy(
            src_ref=idx_ref, dst_ref=bidx.at[row], send_sem=isend.at[n], recv_sem=irecv.at[n],
            device_id=peer, device_id_type=MESH,
        )
        copy.start()
        small.append(copy)
    for n, peer in enumerate(col_peers):
        n = n + len(row_peers)
        copy = pltpu.make_async_remote_copy(
            src_ref=idx_ref, dst_ref=aidx.at[col], send_sem=isend.at[n], recv_sem=irecv.at[n],
            device_id=peer, device_id_type=MESH,
        )
        copy.start()
        small.append(copy)

    a_across = put(a_ref, a_all.at[col], (row, at_x(1, x)))
    b0 = ring(b_src, b_all, at_z, z, 0, up, down)
    a0 = ring(a_src, a_all, at_x, x, 0, east, west)
    b_across = put(b_ref, b_all.at[row], (at_z(1, z), col))
    handed = [put(a_ref, a_all.at[col], twin)]

    b_in = pltpu.make_async_copy(b_ref, b_own, lsem.at[0])
    a_in = pltpu.make_async_copy(a_ref, a_own, lsem.at[1])
    b_in.start()
    a_in.start()
    b_in.wait()
    b_out = pltpu.make_async_copy(b_own, b_all.at[row], lsem.at[2])
    b_out.start()
    a_in.wait()
    a_out = pltpu.make_async_copy(a_own, a_all.at[col], lsem.at[3])
    a_out.start()

    aidx[col] = idx_ref[...]
    bidx[row] = idx_ref[...]
    for copy in small:
        copy.wait_recv()
    build_lists(aidx, bidx, ccol_ref, arep, brep, list_ref)

    def first_hop_near(ring_copies, whole, at, pos, h, plus, minus):
        p0, m1, _, _ = ring_copies
        p0.wait_recv()
        f0 = pass_on(whole, at, pos, h, -1, 0, plus)
        m1.wait_recv()
        f1 = pass_on(whole, at, pos, h, 1, 1, minus)
        return f0, f1

    a0f = first_hop_near(a0, a_all, at_x, x, 0, east, west)
    handed += [a_hand(0, -1, 0), a_hand(0, 1, 1)]
    b0f = first_hop_near(b0, b_all, at_z, z, 0, up, down)
    a0[2].wait_recv()
    a0[3].wait_recv()
    handed += [a_hand(0, -1, 1), a_hand(0, 1, 0)]
    a_across.wait_recv()
    a1 = ring(a_src, a_all, at_x, x, 1, east, west)
    handed += [put(a_all.at[at_x(1, x)], a_all.at[at_x(1, x)], twin)]
    b0[2].wait_recv()
    b0[3].wait_recv()
    b_across.wait_recv()
    b1 = ring(b_src, b_all, at_z, z, 1, up, down)
    a0f[0].wait_recv()
    a0f[1].wait_recv()
    handed += [a_hand(0, 2, 0), a_hand(0, 2, 1)]
    a1f = first_hop_near(a1, a_all, at_x, x, 1, east, west)
    handed += [a_hand(1, -1, 0), a_hand(1, 1, 1)]
    a1[2].wait_recv()
    a1[3].wait_recv()
    handed += [a_hand(1, -1, 1), a_hand(1, 1, 0)]
    b0f[0].wait_recv()
    b0f[1].wait_recv()
    b1f = first_hop_near(b1, b_all, at_z, z, 1, up, down)
    a1f[0].wait_recv()
    a1f[1].wait_recv()
    handed += [a_hand(1, 2, 0), a_hand(1, 2, 1)]
    b1[2].wait_recv()
    b1[3].wait_recv()
    b1f[0].wait_recv()
    b1f[1].wait_recv()
    for copy in handed:
        copy.wait_recv()
    for copy in small + started:
        copy.wait_send()
    b_out.wait()
    a_out.wait()


N_COPIES = 41


def gather(idx, keep, a_vals, b_vals):
    any_space = pl.BlockSpec(memory_space=pl.ANY)
    vmem = pl.BlockSpec(memory_space=pltpu.VMEM)
    return pl.pallas_call(
        gather_kernel,
        name="gather",
        out_shape=(
            jax.ShapeDtypeStruct((N_COL, RB, NZS, BS, BS), jnp.bfloat16),
            jax.ShapeDtypeStruct((N_ROW, RB, NZBC, BS, BS), jnp.bfloat16),
            jax.ShapeDtypeStruct((LIST_ROWS, KEPT), jnp.int32),
        ),
        in_specs=[vmem, vmem, any_space, any_space],
        out_specs=(any_space, any_space, vmem),
        scratch_shapes=[
            pltpu.VMEM((N_COL, 8, 128), jnp.int32),
            pltpu.VMEM((N_ROW, 8, 128), jnp.int32),
            pltpu.VMEM((N_COL, 128), jnp.int32),
            pltpu.VMEM((N_COL, 128), jnp.int32),
            pltpu.VMEM((RB, NZS, BS, BS), jnp.bfloat16),
            pltpu.VMEM((RB, NZBC, BS, BS), jnp.bfloat16),
            pltpu.SemaphoreType.DMA((N_COPIES,)),
            pltpu.SemaphoreType.DMA((N_COPIES,)),
            pltpu.SemaphoreType.DMA((N_ROW + N_COL - 2,)),
            pltpu.SemaphoreType.DMA((N_ROW + N_COL - 2,)),
            pltpu.SemaphoreType.DMA((4,)),
        ],
        compiler_params=pltpu.CompilerParams(collective_id=0, has_side_effects=True),
    )(idx, keep, a_vals, b_vals)


def product_kernel(
    list_ref, order_ref, a_all, b_all, out_ref, a_buf, b_buf, acc, kept, place, a_sem, b_sem, o_sem
):
    def a_copy(i, slot):
        return pltpu.make_async_copy(
            a_all.at[:, i], a_buf.at[slot], a_sem.at[slot]
        )

    b_copy = pltpu.make_async_copy(b_all, b_buf.at[pl.ds(0, ZERO)], b_sem)
    a_copy(0, 0).start()
    b_copy.start()
    b_buf[ZERO] = jnp.zeros((BS, BS), jnp.bfloat16)

    @pl.loop(0, KEPT)
    def _(d):
        place[order_ref[d]] = d

    b_copy.wait()

    @pl.loop(0, RB)
    def _(i):
        slot = i % 2

        @pl.when(i + 1 < RB)
        def _():
            a_copy(i + 1, 1 - slot).start()

        a_copy(i, slot).wait()
        most = list_ref[SLOTS, i * NZC]
        for m in range(1, NZC):
            most = jnp.maximum(most, list_ref[SLOTS, i * NZC + m])
        acc[...] = jnp.zeros_like(acc)

        @pl.loop(0, (most + 1) // 2)
        def _(t):
            for m in range(NZC):
                one = list_ref[2 * t, i * NZC + m]
                two = list_ref[2 * t + 1, i * NZC + m]
                p1, p2 = one // CODE, two // CODE
                left = jnp.concatenate(
                    [a_buf[slot, p1 // NZS, p1 % NZS], a_buf[slot, p2 // NZS, p2 % NZS]], axis=1
                )
                right = jnp.concatenate([b_buf[one % CODE], b_buf[two % CODE]], axis=0)
                acc[m] += jnp.dot(left, right, preferred_element_type=jnp.float32)

        for m in range(NZC):
            o = i * NZC + m
            kept[o] = acc[m].astype(jnp.bfloat16)
            pltpu.make_async_copy(kept.at[o], out_ref.at[place[o]], o_sem).start()

    pltpu.make_async_copy(kept, out_ref, o_sem).wait()


def product(lists, order, a_all, b_all):
    any_space = pl.BlockSpec(memory_space=pl.ANY)
    smem = pl.BlockSpec(memory_space=pltpu.SMEM)
    b_all = b_all.reshape(ZERO, BS, BS)
    return pl.pallas_call(
        product_kernel,
        name="product",
        out_shape=jax.ShapeDtypeStruct((KEPT, BS, BS), jnp.bfloat16),
        in_specs=[smem, smem, any_space, any_space],
        out_specs=any_space,
        scratch_shapes=[
            pltpu.VMEM((2, N_COL, NZS, BS, BS), jnp.bfloat16),
            pltpu.VMEM((ZERO + 1, BS, BS), jnp.bfloat16),
            pltpu.VMEM((NZC, BS, BS), jnp.float32),
            pltpu.VMEM((KEPT, BS, BS), jnp.bfloat16),
            pltpu.SMEM((KEPT,), jnp.int32),
            pltpu.SemaphoreType.DMA((2,)),
            pltpu.SemaphoreType.DMA,
            pltpu.SemaphoreType.DMA,
        ],
    )(lists, order, a_all, b_all)


def on_device(a_vals, a_cols, b_vals, b_cols, c_cols, c_send):
    col = lax.axis_index("col")
    wide = lambda part: jnp.pad(part, ((0, 0), (0, 128 - part.shape[1])))
    b_local = (b_cols - col * SBD).reshape(2, PANEL * NZBC)
    a_local = (a_cols - col * PANEL).reshape(1, RB * NZS)
    idx = jnp.concatenate([wide(b_local), wide(a_local), jnp.zeros((5, 128), jnp.int32)], axis=0)
    keep = (c_cols - col * SBD).reshape(1, KEPT)
    a_all, b_all, lists = gather(idx, keep, a_vals, b_vals)
    outgoing = product(lists, c_send.reshape(KEPT), a_all, b_all)
    return lax.all_to_all(outgoing, ("row", "col"), split_axis=0, concat_axis=0, tiled=True)


def solution(mesh):
    in_specs = (
        P("row", "col", None, None),
        P("row", "col"),
        P("row", "col", None, None),
        P("row", "col"),
        P("row", "col"),
        P("row", "col", None),
    )
    out_specs = P(("row", "col"), None, None)
    return jax.shard_map(
        on_device, mesh=mesh, in_specs=in_specs, out_specs=out_specs, check_vma=False
    )
```

time: 713 us -> 228 us (0.32)
  matrix products: 311 us -> 0 us
  Pallas kernels: 0 us -> 163 us
  local copies, waits for them, and re-layouts: 152 us -> 3.17 us
  waiting for transfers between devices: 124 us -> 0 us
  starting transfers between devices: 23.3 us -> 0 us
  blocking collectives: 80.1 us -> 58.1 us
  between operations: 13.5 us -> 0.03 us
    dot_general x32 -> x0, matrix products: 311 us -> none  [the longest x16 184 us: accumulate(): jnp.einsum('ipab,ipnbc->inac', a_piece, selected, preferred_element_type=...]
    pallas_call x0 -> x2, Pallas kernels: none -> 163 us  [the longest x1 123 us: gather(): pl.pallas_call(gather_kernel, name='gather', out_shape=(jax.ShapeDtypeStr...]
    gather x49 -> x0, local copies, waits for them, and re-layouts: 133 us -> none  [the longest x16 115 us: accumulate(): b_chosen = jnp.take(b_whole, inner_rows, axis=0)]
    all_gather x1 -> x0, waiting for transfers between devices: 124 us -> none  [on_device(): lax.all_gather(b_vals, 'row', axis=0, tiled=True)]
    ppermute x30 -> x0, starting transfers between devices: 23.3 us -> none  [from_behind(): lax.ppermute(shard, axis, [(i, (i + by) % length) for i in range(length)])]
    all_gather x1 -> x0, blocking collectives: 21.8 us -> none  [on_device(): lax.all_gather(local_cols, 'row', axis=0, tiled=True)]
  transfers between devices with their start and end apart: 31 -> 0, of which waited for: 1 -> 0; matrix products, arithmetic and copies ran while one was open for 60% -> 0% of each run, Pallas kernels for 0% -> 0%
where the time goes in v1:
time: 228 us; the launch traced here: 227 us
  Pallas kernels  163 us (71%)
  blocking collectives  58.1 us (25%)
  local copies, waits for them, and re-layouts  3.17 us (1%)
  other arithmetic  2.72 us (1%)
    pallas_call x1, Pallas kernels, gather(): pl.pallas_call(gather_kernel, name='gather', out_shape=(jax.ShapeDtypeStr...  123 us
    all_to_all x1, blocking collectives, on_device(): lax.all_to_all(outgoing, ('row', 'col'), split_axis=0, concat_axis=0, til...  58.1 us
    pallas_call x1, Pallas kernels, product(): pl.pallas_call(product_kernel, name='product', out_shape=jax.ShapeDtypeSt...  40 us

profile of v1, /device:TPU:1, one launch (start us, length us, event | category | flops | bytes accessed | tf_op | source)
XLA Modules:
  0.0 227.3 jit_solution(751632443170113417)
XLA Ops:
  0.0 0.1 pad.12.clone
  0.1 0.7 broadcast_subtract_fusion.1
  0.8 0.7 broadcast_subtract_fusion
  1.5 0.1 copy.12
  1.5 0.7 reshape.17.ccol_ref
  2.2 0.1 copy.10
  2.3 0.1 reshape.15
  2.4 0.7 broadcast_subtract_fusion.2
  3.0 0.1 copy.11
  3.1 0.1 reshape.16
  3.2 0.7 fusion.idx_ref
  3.9 123.3 %gather.1 = (bf16[16,16,2,128,128]{4,3,2,1,0:T(8,128)(2,1)}, bf16[8,16,3,128,128]{4,3,2,1,0:T(8,128)(2,1)}, s32[40,128]{1,0:T(8,128)}) custom-call(s32[8,128]{1,0:T(8,128)} %fusion.idx_ref, s32[1,128]{1,0:T(1,128)} %reshape.17.ccol_ref, bf16[16,2,128,128]{3,2,1,0:T(8,128)(2,1)} %a_ref.1, bf16[16,3,128,128]{3,2,1,0:T(8,128)(2,1)} %b_ref.1), custom_call_target="tpu_custom_call" | custom-call | tf_op jit(solution)/shard_map/gather/pallas_call | solution.py:217
  127.1 40.0 %product.1 = bf16[128,128,128]{2,1,0:T(8,128)(2,1)} custom-call(s32[40,128]{1,0:T(8,128)} %get-tuple-element.8.list_ref, s32[128]{0:T(128)} %bitcast.3, bf16[16,16,2,128,128]{4,3,2,1,0:T(8,128)(2,1)} %get-tuple-element.9.a_all, bf16[384,128,128]{2,1,0:T(8,128)(2,1)} %bitcast.2), custom_call_target="tpu_custom_call" | custom-call | tf_op jit(solution)/shard_map/product/pallas_call | solution.py:301
  167.2 58.1 %all_to_all.5 = bf16[128,128,128]{2,1,0:T(8,128)(2,1)S(1)} all-to-all(bf16[128,128,128]{2,1,0:T(8,128)(2,1)} %product.1), channel_id=1, replica_groups=mesh['row'=8,'col'=16] {'row','col'}, dimensions={0} | all-to-all | bytes 8388608 | tf_op jit(solution)/shard_map/all_to_all | solution.py:329
  225.3 2.0 copy.14
  (1 shorter events, 0.0 us)
